TPU v7x, 32 devices: a whole 2x2x4 slice. The times are simulated.
32 devices in a mesh: dp: 8 (over y, x, core), mp: 4 (over z).
Axes of the slice: x: 2, y: 2, z: 4, core: 2. Of those that a mesh axis runs over, the one named last changes fastest.
Arguments:
- tokens: bfloat16 [64, 256, 1024], P(('dp', 'mp')), may hold values from -6 to 6
- cotangent: bfloat16 [64, 256, 1024], P(('dp', 'mp')), may hold values from -6 to 6
- w_qkv: bfloat16 [3, 1024, 1024], P(None, None, 'mp'), may hold values from -0.1875 to 0.1875
- w_out: bfloat16 [1024, 1024], P('mp'), may hold values from -1 to 1
- w_up: bfloat16 [1024, 4096], P(None, 'mp'), may hold values from -0.1875 to 0.1875
- w_down: bfloat16 [4096, 1024], P('mp'), may hold values from -0.09375 to 0.09375
- w_mod: bfloat16 [1024, 6144], P('mp'), may hold values from -0.1875 to 0.1875
- b_mod: bfloat16 [6, 1024], replicated, may hold values from -3 to 3
- time_weight: bfloat16 [256, 1024], P(None, 'mp'), may hold values from -0.375 to 0.375
- class_table: bfloat16 [1000, 1024], P(None, 'mp'), may hold values from -6 to 6
- rel_table: bfloat16 [16, 961], P('mp'), may hold values from -5 to 5
- window_step: int32 [64], P('dp'), may hold values from 0 to 999
- window_label: int32 [64], P('dp'), may hold values from 0 to 999
- window_cols: int32 [64], P('dp'), may hold values from 0 to 16, as said below
Outputs:
- block_out: bfloat16 [64, 256, 1024], P(('dp', 'mp'))
- tokens_grad: bfloat16 [64, 256, 1024], P(('dp', 'mp'))
- w_qkv_grad: float32 [3, 1024, 1024], P(None, None, 'mp')
- w_out_grad: float32 [1024, 1024], P('mp')
- w_up_grad: float32 [1024, 4096], P(None, 'mp')
- w_down_grad: float32 [4096, 1024], P('mp')
- w_mod_grad: float32 [1024, 6144], P('mp')
- b_mod_grad: float32 [6, 1024], replicated
- time_weight_grad: float32 [256, 1024], P(None, 'mp')
- class_table_grad: float32 [1000, 1024], P(None, 'mp')
- rel_table_grad: float32 [16, 961], P('mp')
Inputs may be any that keep to these rules, and one draw needn't show every extreme that they name: `window_cols`: within each aligned block of 8 windows the used slots (nonzero entry) come first, two or more of them; some block is used in full. A used slot holds 16 or 8 valid columns, an unused one 0.
All inputs are finite; a program needn't handle non-finite values.
Results may differ from a plain program's by a relative error of at most 0.028.
Values may be sent and summed in bfloat16 or wider, within the bound.
No kernel may reach another device: no remote copies, remote signals or barrier semaphores. Data moves between devices by JAX's collectives and lax.ppermute only.
A program may use at most 192 MiB of HBM per device.

v0:
```python
import math
import jax
import jax.numpy as jnp
from jax import lax
from jax.sharding import PartitionSpec as P

HEAD_DIM = 64
WSIDE = 16
FREQ = 256
EPS = 1e-06
HIGH = lax.Precision.HIGHEST
MASKED = -1000000000.0


def exact(matrix_a, matrix_b):
    return jnp.dot(matrix_a, matrix_b, precision=HIGH, preferred_element_type=jnp.float32)


def layer_norm(field):
    center = field - jnp.mean(field, axis=-1, keepdims=True)
    spread = jnp.mean(center * center, axis=-1, keepdims=True)
    return center * lax.rsqrt(spread + EPS)


def modulate(field, scale_part, shift_part):
    return layer_norm(field) * (1.0 + scale_part) + shift_part


def gelu_tanh(field):
    return jax.nn.gelu(field, approximate=True)


def step_features(step_ids, half_width):
    frequency = jnp.exp(-math.log(10000.0) * jnp.arange(half_width, dtype=jnp.float32) / half_width)
    angles = step_ids.astype(jnp.float32)[:, None] * frequency[None, :]
    return jnp.concatenate([jnp.cos(angles), jnp.sin(angles)], axis=1)


def offset_table(window_side):
    offsets = jnp.arange(window_side, dtype=jnp.int32)
    offset_diff = offsets[:, None] - offsets[None, :] + window_side - 1
    return (
        offset_diff[None] == jnp.arange(2 * window_side - 1, dtype=jnp.int32)[:, None, None]
    ).astype(jnp.float32)


def make_scores(queries, keys, rel_bias, keep_keys, score_scale):
    raw_scores = (
        jnp.einsum("wihd,wjhd->whij", queries, keys, preferred_element_type=jnp.float32)
        * score_scale
        + rel_bias[None]
    )
    return jnp.where(keep_keys[:, None, None, :], raw_scores, MASKED)


def per_device(
    tokens,
    cotangent,
    w_qkv,
    w_out,
    w_up,
    w_down,
    w_mod,
    b_mod,
    time_weight,
    class_table,
    rel_table,
    window_step,
    window_label,
    window_cols,
):
    own_count, win_tok, width = tokens.shape
    group_size = window_step.shape[0]
    local_heads = w_out.shape[0] // HEAD_DIM
    score_scale = HEAD_DIM ** (-0.5)
    first_own = lax.axis_index("mp") * own_count
    features = step_features(window_step, FREQ // 2).astype(jnp.bfloat16)
    classes = jnp.arange(class_table.shape[0], dtype=jnp.int32)
    onehot = (window_label[:, None] == classes[None, :]).astype(jnp.bfloat16)
    cond_pre = jnp.dot(features, time_weight, preferred_element_type=jnp.float32) + jnp.dot(
        onehot, class_table, preferred_element_type=jnp.float32
    )
    condition = jax.nn.silu(cond_pre).astype(jnp.bfloat16)
    partial_mod = jnp.dot(condition, w_mod, preferred_element_type=jnp.float32)
    modulation = (
        lax.psum(partial_mod, "mp").reshape(group_size, 6, width) + b_mod.astype(jnp.float32)[None]
    )
    own_mod = lax.dynamic_slice_in_dim(modulation, first_own, own_count, 0)
    shift_attn, scale_attn, gate_attn, shift_mlp, scale_mlp, gate_mlp = [
        own_mod[:, column][:, None, :] for column in range(6)
    ]
    token_cols = jnp.arange(win_tok, dtype=jnp.int32) % WSIDE
    keep_keys = token_cols[None, :] < window_cols[:, None]
    keep_rows = lax.dynamic_slice_in_dim(keep_keys, first_own, own_count, 0)[:, :, None]
    rel_span = 2 * WSIDE - 1
    offset_pick = offset_table(WSIDE)
    rel_grid = rel_table.astype(jnp.float32).reshape(local_heads, rel_span, rel_span)
    half_bias = jnp.einsum("ayz,hab->hyzb", offset_pick, rel_grid, precision=HIGH)
    rel_bias = jnp.einsum("hyzb,bxw->hyxzw", half_bias, offset_pick, precision=HIGH).reshape(
        local_heads, win_tok, win_tok
    )
    inputs = tokens.astype(jnp.float32)
    normed_attn = modulate(inputs, scale_attn, shift_attn).astype(jnp.bfloat16)
    gathered_attn = lax.all_gather(normed_attn, "mp", axis=0, tiled=True)
    projected = jnp.einsum(
        "wtd,kde->kwte", gathered_attn, w_qkv, preferred_element_type=jnp.float32
    ).astype(jnp.bfloat16)
    split_shape = (group_size, win_tok, local_heads, HEAD_DIM)
    queries = projected[0].reshape(split_shape)
    keys = projected[1].reshape(split_shape)
    values = projected[2].reshape(split_shape)
    scores = make_scores(queries, keys, rel_bias, keep_keys, score_scale)
    row_max = jnp.max(scores, axis=-1, keepdims=True)
    log_total = row_max + jnp.log(jnp.sum(jnp.exp(scores - row_max), axis=-1, keepdims=True))
    probs_low = jnp.exp(scores - log_total).astype(jnp.bfloat16)
    attended = (
        jnp.einsum("whij,wjhd->wihd", probs_low, values, preferred_element_type=jnp.float32)
        .astype(jnp.bfloat16)
        .reshape(group_size, win_tok, local_heads * HEAD_DIM)
    )
    row_block = attended
    branch = lax.psum_scatter(
        jnp.einsum("wte,ed->wtd", row_block, w_out, preferred_element_type=jnp.float32).astype(
            jnp.bfloat16
        ),
        "mp",
        scatter_dimension=0,
        tiled=True,
    ).astype(jnp.float32)
    middle = inputs + gate_attn * branch
    normed_mlp = modulate(middle, scale_mlp, shift_mlp).astype(jnp.bfloat16)
    gathered_mlp = lax.all_gather(normed_mlp, "mp", axis=0, tiled=True)
    hidden_pre = jnp.einsum("wtd,df->wtf", gathered_mlp, w_up, preferred_element_type=jnp.float32)
    activation = gelu_tanh(hidden_pre).astype(jnp.bfloat16)
    row_block = activation
    mlp_out = lax.psum_scatter(
        jnp.einsum("wtf,fd->wtd", row_block, w_down, preferred_element_type=jnp.float32).astype(
            jnp.bfloat16
        ),
        "mp",
        scatter_dimension=0,
        tiled=True,
    ).astype(jnp.float32)
    block_out = jnp.where(keep_rows, middle + gate_mlp * mlp_out, 0.0).astype(jnp.bfloat16)
    grad_rows = jnp.where(keep_rows, cotangent.astype(jnp.float32), 0.0)
    d_gate_mlp = jnp.sum(grad_rows * mlp_out, axis=1)
    d_mlp = (gate_mlp * grad_rows).astype(jnp.bfloat16)
    d_mlp_all = lax.all_gather(d_mlp, "mp", axis=0, tiled=True)
    normed_again = lax.all_gather(normed_mlp, "mp", axis=0, tiled=True)
    pre_again = jnp.einsum("wtd,df->wtf", normed_again, w_up, preferred_element_type=jnp.float32)
    act_again = gelu_tanh(pre_again).astype(jnp.bfloat16)
    w_down_grad = jnp.einsum(
        "wtf,wtd->fd", act_again, d_mlp_all, preferred_element_type=jnp.float32
    )
    d_act = jnp.einsum("wtd,fd->wtf", d_mlp_all, w_down, preferred_element_type=jnp.float32)
    d_hidden = jax.vjp(gelu_tanh, pre_again)[1](d_act)[0].astype(jnp.bfloat16)
    w_up_grad = jnp.einsum(
        "wtd,wtf->df", normed_again, d_hidden, preferred_element_type=jnp.float32
    )
    row_block = d_hidden
    d_normed_mlp = lax.psum_scatter(
        jnp.einsum("wtf,df->wtd", row_block, w_up, preferred_element_type=jnp.float32),
        "mp",
        scatter_dimension=0,
        tiled=True,
    )
    pull_mlp = jax.vjp(modulate, middle, scale_mlp, shift_mlp)[1]
    d_middle_norm, d_scale_mlp, d_shift_mlp = pull_mlp(d_normed_mlp)
    d_middle = grad_rows + d_middle_norm
    d_gate_attn = jnp.sum(d_middle * branch, axis=1)
    d_branch = (gate_attn * d_middle).astype(jnp.bfloat16)
    d_branch_all = lax.all_gather(d_branch, "mp", axis=0, tiled=True)
    w_out_grad = jnp.einsum(
        "wte,wtd->ed", attended, d_branch_all, preferred_element_type=jnp.float32
    )
    d_attended = (
        jnp.einsum("wtd,ed->wte", d_branch_all, w_out, preferred_element_type=jnp.float32)
        .astype(jnp.bfloat16)
        .reshape(split_shape)
    )
    probs_back = jnp.exp(make_scores(queries, keys, rel_bias, keep_keys, score_scale) - log_total)
    d_probs = jnp.einsum("wihd,wjhd->whij", d_attended, values, preferred_element_type=jnp.float32)
    d_values = jnp.einsum(
        "whij,wihd->wjhd",
        probs_back.astype(jnp.bfloat16),
        d_attended,
        preferred_element_type=jnp.float32,
    ).astype(jnp.bfloat16)
    row_delta = jnp.sum(probs_back * d_probs, axis=-1, keepdims=True)
    d_scores = (probs_back * (d_probs - row_delta)).astype(jnp.bfloat16)
    d_queries = (
        jnp.einsum("whij,wjhd->wihd", d_scores, keys, preferred_element_type=jnp.float32)
        * score_scale
    ).astype(jnp.bfloat16)
    d_keys = (
        jnp.einsum("whij,wihd->wjhd", d_scores, queries, preferred_element_type=jnp.float32)
        * score_scale
    ).astype(jnp.bfloat16)
    d_bias = jnp.sum(d_scores, axis=0, dtype=jnp.float32).reshape(
        local_heads, WSIDE, WSIDE, WSIDE, WSIDE
    )
    d_half = jnp.einsum("hyxzw,bxw->hyzb", d_bias, offset_pick, precision=HIGH)
    rel_table_grad = jnp.einsum("hyzb,ayz->hab", d_half, offset_pick, precision=HIGH).reshape(
        local_heads, rel_span * rel_span
    )
    d_projected = jnp.stack([d_queries, d_keys, d_values]).reshape(
        3, group_size, win_tok, local_heads * HEAD_DIM
    )
    w_qkv_grad = jnp.einsum(
        "wtd,kwte->kde", gathered_attn, d_projected, preferred_element_type=jnp.float32
    )
    row_block = d_projected
    d_normed_attn = lax.psum_scatter(
        jnp.einsum("kwte,kde->wtd", row_block, w_qkv, preferred_element_type=jnp.float32).astype(
            jnp.bfloat16
        ),
        "mp",
        scatter_dimension=0,
        tiled=True,
    ).astype(jnp.float32)
    pull_attn = jax.vjp(modulate, inputs, scale_attn, shift_attn)[1]
    d_inputs_norm, d_scale_attn, d_shift_attn = pull_attn(d_normed_attn)
    tokens_grad = (d_middle + d_inputs_norm).astype(jnp.bfloat16)
    d_mod_own = jnp.stack(
        [
            d_shift_attn[:, 0],
            d_scale_attn[:, 0],
            d_gate_attn,
            d_shift_mlp[:, 0],
            d_scale_mlp[:, 0],
            d_gate_mlp,
        ],
        axis=1,
    ).reshape(own_count, 6 * width)
    d_modulation = lax.all_gather(d_mod_own.astype(jnp.bfloat16), "mp", axis=0, tiled=True).astype(
        d_mod_own.dtype
    )
    d_condition = exact(d_modulation, w_mod.T)
    d_cond_pre = jax.vjp(jax.nn.silu, cond_pre)[1](d_condition)[0]
    time_weight_grad = exact(features.astype(jnp.float32).T, d_cond_pre)
    class_table_grad = exact(onehot.astype(jnp.float32).T, d_cond_pre)
    w_mod_grad = exact(condition.astype(jnp.float32).T, d_modulation)
    b_mod_grad = jnp.sum(d_modulation, axis=0).reshape(6, width)
    (
        w_qkv_grad,
        w_out_grad,
        w_up_grad,
        w_down_grad,
        w_mod_grad,
        b_mod_grad,
        time_weight_grad,
        class_table_grad,
        rel_table_grad,
    ) = lax.psum(
        (
            w_qkv_grad,
            w_out_grad,
            w_up_grad,
            w_down_grad,
            w_mod_grad,
            b_mod_grad,
            time_weight_grad,
            class_table_grad,
            rel_table_grad,
        ),
        "dp",
    )
    return (
        block_out,
        tokens_grad,
        w_qkv_grad,
        w_out_grad,
        w_up_grad,
        w_down_grad,
        w_mod_grad,
        b_mod_grad,
        time_weight_grad,
        class_table_grad,
        rel_table_grad,
    )


def solution(mesh):
    return jax.shard_map(
        per_device,
        mesh=mesh,
        in_specs=(
            P(("dp", "mp"), None, None),
            P(("dp", "mp"), None, None),
            P(None, None, "mp"),
            P("mp", None),
            P(None, "mp"),
            P("mp", None),
            P("mp", None),
            P(),
            P(None, "mp"),
            P(None, "mp"),
            P("mp", None),
            P("dp"),
            P("dp"),
            P("dp"),
        ),
        out_specs=(
            P(("dp", "mp"), None, None),
            P(("dp", "mp"), None, None),
            P(None, None, "mp"),
            P("mp", None),
            P(None, "mp"),
            P("mp", None),
            P("mp", None),
            P(),
            P(None, "mp"),
            P(None, "mp"),
            P("mp", None),
        ),
        check_vma=False,
    )
```

profile of v0, /device:TPU:0, one launch (start us, length us, event | category | flops | bytes accessed | tf_op | source)
XLA Modules:
  0.0 1149.7 jit_solution(5632088591709699951)
XLA Ops:
  11.8 1.4 convert_reduce_fusion.1
  13.2 1.6 fusion.28
  14.9 34.8 %all-reduce.5.cloned.1.call-done = f32[8,6,1024]{2,0,1:T(8,128)} async-done(((f32[8,6,1024]{2,0,1:T(8,128)}), f32[8,6,1024]{2,0,1:T(8,128)}) %all-reduce.5.cloned.1.call-update) | async-done | bytes 196624 | tf_op jit(solution)/shard_map/psum | solution.py:86
  50.6 2.7 fusion.21
  54.1 5.6 convolution_bitcast_fusion
  59.8 12.0 %copy.103 = f32[4,16,16,16,16]{2,1,4,3,0:T(8,128)} copy(f32[4,16,16,16,16]{3,4,1,0,2:T(8,128)} %convolution_bitcast_fusion) | data formatting | bytes 2097152 | tf_op jit(solution)/shard_map/add | solution.py:49
  71.8 7.0 reshape.213
  78.9 55.0 %all-gather.6.cloned.1.call-done = bf16[8,256,1024]{2,1,0:T(8,128)(2,1)} async-done(((bf16[2,256,1024]{2,1,0:T(8,128)(2,1)}), bf16[8,256,1024]{2,1,0:T(8,128)(2,1)}) %all-gather.6.cloned.1.call-update) | async-done | bytes 4194320 | tf_op jit(solution)/shard_map/all_gather | solution.py:104
  133.9 6.1 convert_bitcast_fusion
  141.4 2.9 fusion.83
  144.3 1.7 exponential_reduce_fusion
  146.0 1.5 copy-done.1
  147.5 1.4 convolution_convert_fusion.4
  149.9 3.3 convolution_convert_fusion.1
  153.3 75.4 %reduce-scatter.5.cloned.1.call-done = bf16[2,256,1024]{2,1,0:T(8,128)(2,1)} async-done(((bf16[8,256,1024]{2,1,0:T(8,128)(2,1)}), bf16[2,256,1024]{2,1,0:T(8,128)(2,1)}) %reduce-scatter.5.cloned.1.call-update) | async-done | bytes 1048592 | tf_op jit(solution)/shard_map/reduce_scatter | solution.py:122
  228.7 2.1 fusion.40
  230.8 2.1 multiply_reduce_fusion.3
  233.0 1.6 add_convert_fusion.1
  234.7 2.5 multiply_convert_fusion.5
  237.2 78.7 %all-gather.8.cloned.1.call-done = bf16[8,256,1024]{2,1,0:T(8,128)(2,1)} async-done(((bf16[2,256,1024]{2,1,0:T(8,128)(2,1)}), bf16[8,256,1024]{2,1,0:T(8,128)(2,1)}) %all-gather.8.cloned.1.call-update) | async-done | bytes 4194320 | tf_op jit(solution)/shard_map/all_gather | solution.py:132
  316.0 10.9 fusion.34
  326.9 70.4 %all-gather.10.cloned.1.call-done = bf16[8,256,1024]{2,1,0:T(8,128)(2,1)} async-done(((bf16[2,256,1024]{2,1,0:T(8,128)(2,1)}), bf16[8,256,1024]{2,1,0:T(8,128)(2,1)}) %all-gather.10.cloned.1.call-update) | async-done | bytes 4194320 | tf_op jit(solution)/shard_map/all_gather | solution.py:148
  397.2 12.8 %fusion.6 = bf16[8,256,1024]{2,1,0:T(8,128)(2,1)S(1)} fusion(f32[8,256,1024]{2,1,0:T(8,128)} %fusion.34, bf16[8,256,1024]{2,1,0:T(8,128)(2,1)} %all-gather.10.cloned.1.call-done, bf16[1024,1024]{1,0:T(8,128)(2,1)} %param.19), kind=kOutput, calls=%fused_computation.8 | convolution fusion | flops 4336910336 | bytes 18874368 | tf_op jit(solution)/shard_map/wtd,fd->wtf/dot_general | solution.py:155
  410.0 2.0 copy-done.35
  412.0 7.0 fusion.32
  419.1 143.2 %reduce-scatter.9.cloned.1.call-done = f32[2,256,1024]{2,1,0:T(8,128)} async-done(((f32[8,256,1024]{2,1,0:T(8,128)}), f32[2,256,1024]{2,1,0:T(8,128)}) %reduce-scatter.9.cloned.1.call-update) | async-done | bytes 2097168 | tf_op jit(solution)/shard_map/reduce_scatter | solution.py:161
  562.3 3.3 multiply_reduce_fusion.1
  566.7 1.3 copy-done.6
  568.1 1.4 multiply_convert_fusion.4
  569.6 81.5 %all-gather.12.cloned.1.call-done = bf16[8,256,1024]{2,1,0:T(8,128)(2,1)} async-done(((bf16[2,256,1024]{2,1,0:T(8,128)(2,1)}), bf16[8,256,1024]{2,1,0:T(8,128)(2,1)}) %all-gather.12.cloned.1.call-update) | async-done | bytes 4194320 | tf_op jit(solution)/shard_map/all_gather | solution.py:172
  651.0 3.7 convolution_convert_fusion.3
  654.8 6.0 convolution_convert_fusion.2
  660.8 2.5 multiply_reduce_fusion
  663.3 3.9 convert_reduce_fusion
  667.2 2.4 multiply_convert_fusion.2
  669.5 1.8 multiply_convert_fusion.3
  671.4 2.3 copy.79
  673.6 2.2 copy.77
  675.9 2.3 copy.78
  678.1 7.8 bitcast_convert_fusion
  686.0 11.5 %convolution_convert_fusion = bf16[8,256,1024]{2,1,0:T(8,128)(2,1)} fusion(bf16[1024,1024]{1,0:T(8,128)(2,1)} %param.19, f32[8,256,1024]{2,1,0:T(8,128)} %fusion.34), kind=kOutput, calls=%fused_computation.34 | convolution fusion | flops 4315938816 | bytes 14680064 | tf_op jit(solution)/shard_map/wtf,fd->wtd/dot_general | solution.py:137
  697.8 10.2 convolution_bitcast_fusion.2
  708.1 11.2 convolution_bitcast_fusion.1
  719.3 2.3 convolution_bitcast_fusion.3
  722.8 5.5 fusion.36
  728.3 33.1 %reduce-scatter.11.cloned.1.call-done = bf16[2,256,1024]{2,1,0:T(8,128)(2,1)} async-done(((bf16[8,256,1024]{2,1,0:T(8,128)(2,1)}), bf16[2,256,1024]{2,1,0:T(8,128)(2,1)}) %reduce-scatter.11.cloned.1.call-update) | async-done | bytes 1048592 | tf_op jit(solution)/shard_map/reduce_scatter | solution.py:213
  761.4 1.4 reduce
  762.9 2.1 fusion.29
  765.0 2.7 fusion.27
  767.7 74.0 %reduce-scatter.7.cloned.1.call-done = bf16[2,256,1024]{2,1,0:T(8,128)(2,1)} async-done(((bf16[8,256,1024]{2,1,0:T(8,128)(2,1)}), bf16[2,256,1024]{2,1,0:T(8,128)(2,1)}) %reduce-scatter.7.cloned.1.call-update) | async-done | bytes 1048592 | tf_op jit(solution)/shard_map/reduce_scatter | solution.py:136
  841.6 5.2 fusion.26
  847.0 13.8 %all-gather = bf16[4,2,6144]{2,1,0:T(2,128)(2,1)S(1)} all-gather(bf16[1,2,6144]{2,1,0:T(2,128)(2,1)S(1)} %bitcast.178), channel_id=1, replica_groups=mesh['dp'=8,'mp'=4] {'mp'}, dimensions={0}, use_global_device_ids=true | all-gather | bytes 122880 | tf_op jit(solution)/shard_map/all_gather | solution.py:235
  862.8 1.7 fusion.60
  864.4 3.7 fusion.77
  869.0 6.2 reshape.189
  875.2 6.8 convolution_bitcast_fusion.5
  882.7 25.6 %all-reduce = (f32[6,1024]{1,0:T(8,128)}, f32[4,961]{1,0:T(4,128)}) all-reduce(f32[6,1024]{1,0:T(8,128)S(1)} %reshape.188, f32[4,961]{1,0:T(4,128)S(1)} %reshape.190), channel_id=1, replica_groups=mesh['dp'=8,'mp'=4] {'dp'}, use_global_device_ids=true, to_apply=%region_28.29 | all-reduce | flops 9988 | bytes 79904 | tf_op jit(solution)/shard_map/psum | solution.py:254
  908.3 215.6 %all-reduce.7.cloned.1.call-done = (f32[3,1024,256]{1,2,0:T(8,128)}, f32[256,1024]{1,0:T(8,128)}, f32[1024,1024]{1,0:T(8,128)}, f32[1024,1024]{1,0:T(8,128)}, f3...) async-done(((f32[3,1024,256]{1,2,0:T(8,128)}, f32[256,1024]{1,0:T(8,128)}, f32[1024,1024]{1,0:T(8,128)}, f32[1024,1024]{1,0:T(8,128)}, ...) | async-done | bytes 20160528 | tf_op jit(solution)/shard_map/psum | solution.py:254
  1123.8 3.5 copy.85
  1127.4 2.3 copy.124
  1129.7 5.1 copy.125
  1134.8 2.1 copy.126
  1136.9 1.4 slice-done.3
  1138.3 2.7 copy.127
  (140 shorter events, 17.0 us)
Async XLA Ops:
  7.2 3.3 copy-start
  7.2 42.5 %all-reduce.5.cloned.1.call-start = ((), (), s32[]{:S(2)}) async-start(), calls=%async_computation.4 | async-start | bytes 393216 | tf_op jit(solution)/shard_map/psum | solution.py:86
  8.2 6.7 copy-start.27
  11.7 41.7 %copy-start.28 = (bf16[4,961]{1,0:T(4,128)(2,1)S(1)}, bf16[4,961]{1,0:T(4,128)(2,1)}, u32[]{:S(2)}) copy-start(bf16[4,961]{1,0:T(4,128)(2,1)} %param.24) | copy-start | bytes 23068
  11.7 122.2 %all-gather.6.cloned.1.call-start = ((), (), s32[]{:S(2)}) async-start(), calls=%async_computation.5 | async-start | bytes 5242880 | tf_op jit(solution)/shard_map/all_gather | solution.py:104
  53.3 175.4 %reduce-scatter.5.cloned.1.call-start = ((), (), s32[]{:S(2)}) async-start(), calls=%async_computation.6 | async-start | bytes 5242880 | tf_op jit(solution)/shard_map/reduce_scatter | solution.py:122
  53.5 0.6 copy-start.25
  71.8 7.0 copy-start.30
  140.0 1.4 copy-start.15
  140.3 4.0 copy-start.7
  140.3 4.0 copy-start.12
  140.3 5.7 copy-start.9
  144.3 3.2 copy-start.1
  147.5 2.4 copy-start.23
  149.0 1.0 copy-start.17
  153.3 162.7 %all-gather.8.cloned.1.call-start = ((), (), s32[]{:S(2)}) async-start(), calls=%async_computation.7 | async-start | bytes 5242880 | tf_op jit(solution)/shard_map/all_gather | solution.py:132
  228.7 4.2 copy-start.2
  228.7 4.2 copy-start.4
  234.6 162.6 %all-gather.10.cloned.1.call-start = ((), (), s32[]{:S(2)}) async-start(), calls=%async_computation.9 | async-start | bytes 5242880 | tf_op jit(solution)/shard_map/all_gather | solution.py:148
  237.2 325.1 %reduce-scatter.9.cloned.1.call-start = ((), (), s32[]{:S(2)}) async-start(), calls=%async_computation.10 | async-start | bytes 10485760 | tf_op jit(solution)/shard_map/reduce_scatter | solution.py:161
  397.2 14.8 %copy-start.34 = (bf16[1024,1024]{1,0:T(8,128)(2,1)S(1)}, bf16[1024,1024]{1,0:T(8,128)(2,1)}, u32[]{:S(2)}) copy-start(bf16[1024,1024]{1,0:T(8,128)(2,1)} %param.18) | copy-start | bytes 6291460
  410.0 2.0 copy-start.35
  419.0 232.0 %all-gather.12.cloned.1.call-start = ((), (), s32[]{:S(2)}) async-start(), calls=%async_computation.11 | async-start | bytes 5242880 | tf_op jit(solution)/shard_map/all_gather | solution.py:172
  562.3 3.3 copy-start.3
  562.3 3.4 copy-start.5
  562.3 3.5 copy-start.14
  565.8 2.3 copy-start.11
  566.7 1.4 copy-start.6
  569.5 191.9 %reduce-scatter.11.cloned.1.call-start = ((), (), s32[]{:S(2)}) async-start(), calls=%async_computation.12 | async-start | bytes 5242880 | tf_op jit(solution)/shard_map/reduce_scatter | solution.py:213
  651.0 9.7 slice-start
  654.8 6.0 slice-start.1
  654.8 6.0 copy-start.10
  663.3 3.9 copy-start.13
  667.2 2.4 copy-start.8
  686.0 155.7 %reduce-scatter.7.cloned.1.call-start = ((), (), s32[]{:S(2)}) async-start(), calls=%async_computation.8 | async-start | bytes 5242880 | tf_op jit(solution)/shard_map/reduce_scatter | solution.py:136
  697.6 426.2 %all-reduce.7.cloned.1.call-start = ((), (), s32[]{:S(2)}) async-start(), calls=%async_computation.13 | async-start | bytes 40321024 | tf_op jit(solution)/shard_map/psum | solution.py:254
  697.8 10.2 copy-start.32
  708.1 11.2 copy-start.18
  708.1 11.2 copy-start.33
  719.3 2.3 copy-start.19
  719.3 2.3 copy-start.20
  719.3 2.3 copy-start.21
  719.3 3.6 copy-start.31
  846.9 15.9 %copy-start.29 = (s32[8]{0:T(128)S(1)}, s32[8]{0:T(128)}, u32[]{:S(2)}) copy-start(s32[8]{0:T(128)} %param.26) | copy-start | bytes 100
  868.2 0.7 copy-start.26
  1129.7 5.1 copy-start.16
  1129.7 7.2 slice-start.2
  1134.8 3.5 slice-start.3
  1138.3 2.7 copy-start.24
  1138.3 3.4 copy-start.22
Sparse Core Ops, SparseCore 0:
  11.9 37.7 all-reduce.4
  53.5 80.3 all-gather.5
  153.4 75.2 reduce-scatter.4
  234.7 81.2 all-gather.7
  318.0 79.2 all-gather.9
  419.2 143.0 reduce-scatter.8
  569.6 81.3 all-gather.11
  686.1 75.2 reduce-scatter.10
  764.3 77.2 reduce-scatter.6
  868.3 255.4 all-reduce.6
where the time goes:
time: 1160 us; the launch traced here: 1150 us
  waiting for transfers between devices  862 us (74%)
  matrix products  133 us (11%)
  local copies, waits for them, and re-layouts  60.8 us (5%)
  blocking collectives  39.4 us (3%)
  other arithmetic  38.9 us (3%)
  between operations  14.9 us (1%)
    psum x1, waiting for transfers between devices, per_device(): lax.psum((w_qkv_grad, w_out_grad, w_up_grad, w_down_grad, w_mod_grad, b_m...  216 us
    reduce_scatter x1, waiting for transfers between devices, per_device(): lax.psum_scatter(jnp.einsum('wtf,df->wtd', row_block, w_up, preferred_ele...  143 us
    all_gather x1, waiting for transfers between devices, per_device(): d_branch_all = lax.all_gather(d_branch, 'mp', axis=0, tiled=True)  81.5 us
    all_gather x1, waiting for transfers between devices, per_device(): gathered_mlp = lax.all_gather(normed_mlp, 'mp', axis=0, tiled=True)  78.7 us
    reduce_scatter x1, waiting for transfers between devices, per_device(): lax.psum_scatter(jnp.einsum('wte,ed->wtd', row_block, w_out, preferred_el...  75.4 us
    reduce_scatter x1, waiting for transfers between devices, per_device(): lax.psum_scatter(jnp.einsum('wtf,fd->wtd', row_block, w_down, preferred_e...  74 us
    all_gather x1, waiting for transfers between devices, per_device(): d_mlp_all = lax.all_gather(d_mlp, 'mp', axis=0, tiled=True)  70.4 us
    all_gather x1, waiting for transfers between devices, per_device(): gathered_attn = lax.all_gather(normed_attn, 'mp', axis=0, tiled=True)  55 us
  transfers between devices with their start and end apart: 10, of which 10 were waited for; matrix products, arithmetic and copies ran while one was open for 9% of the time, Pallas kernels for 0%

commit v1 on v0

--- a/solution.py
+++ b/solution.py
@@ -83,7 +83,8 @@
     condition = jax.nn.silu(cond_pre).astype(jnp.bfloat16)
     partial_mod = jnp.dot(condition, w_mod, preferred_element_type=jnp.float32)
     modulation = (
-        lax.psum(partial_mod, "mp").reshape(group_size, 6, width) + b_mod.astype(jnp.float32)[None]
+        jnp.sum(lax.all_gather(partial_mod, "mp"), axis=0).reshape(group_size, 6, width)
+        + b_mod.astype(jnp.float32)[None]
     )
     own_mod = lax.dynamic_slice_in_dim(modulation, first_own, own_count, 0)
     shift_attn, scale_attn, gate_attn, shift_mlp, scale_mlp, gate_mlp = [

time: 1160 us -> 1140 us (0.983)
  waiting for transfers between devices: 862 us -> 826 us
  blocking collectives: 39.4 us -> 61 us
    psum x1 -> x0, waiting for transfers between devices: 34.8 us -> none  [per_device(): lax.psum(partial_mod, 'mp').reshape(group_size, 6, width)]
    all_gather x0 -> x1, blocking collectives: none -> 21.4 us  [per_device(): lax.all_gather(partial_mod, 'mp')]
    unnamed x93 -> x91, local copies, waits for them, and re-layouts: 28.4 us -> 28.4 us
  transfers between devices with their start and end apart: 10 -> 9, of which waited for: 10 -> 9; matrix products, arithmetic and copies ran while one was open for 9% -> 9% of each run, Pallas kernels for 0% -> 0%
where the time goes in v1:
time: 1140 us; the launch traced here: 1130 us
  waiting for transfers between devices  826 us (72%)
  matrix products  133 us (12%)
  blocking collectives  61 us (5%)
  local copies, waits for them, and re-layouts  60.7 us (5%)
  other arithmetic  38.9 us (3%)
  between operations  14.6 us (1%)
    psum x1, waiting for transfers between devices, per_device(): lax.psum((w_qkv_grad, w_out_grad, w_up_grad, w_down_grad, w_mod_grad, b_m...  215 us
    reduce_scatter x1, waiting for transfers between devices, per_device(): lax.psum_scatter(jnp.einsum('wtf,df->wtd', row_block, w_up, preferred_ele...  143 us
    all_gather x1, waiting for transfers between devices, per_device(): d_branch_all = lax.all_gather(d_branch, 'mp', axis=0, tiled=True)  81.5 us
    all_gather x1, waiting for transfers between devices, per_device(): gathered_mlp = lax.all_gather(normed_mlp, 'mp', axis=0, tiled=True)  78.7 us
    reduce_scatter x1, waiting for transfers between devices, per_device(): lax.psum_scatter(jnp.einsum('wte,ed->wtd', row_block, w_out, preferred_el...  75.4 us
    reduce_scatter x1, waiting for transfers between devices, per_device(): lax.psum_scatter(jnp.einsum('wtf,fd->wtd', row_block, w_down, preferred_e...  73.9 us
    all_gather x1, waiting for transfers between devices, per_device(): d_mlp_all = lax.all_gather(d_mlp, 'mp', axis=0, tiled=True)  70.4 us
    all_gather x1, waiting for transfers between devices, per_device(): gathered_attn = lax.all_gather(normed_attn, 'mp', axis=0, tiled=True)  54.7 us
  transfers between devices with their start and end apart: 9, of which 9 were waited for; matrix products, arithmetic and copies ran while one was open for 9% of the time, Pallas kernels for 0%

profile of v1, /device:TPU:0, one launch (start us, length us, event | category | flops | bytes accessed | tf_op | source)
XLA Modules:
  0.0 1134.9 jit_solution(18147087084932094427)
XLA Ops:
  8.1 1.5 convert_reduce_fusion.1
  9.6 1.6 fusion.28
  14.9 21.4 %all-gather = f32[32,6144]{1,0:T(8,128)S(1)} all-gather(f32[8,6144]{1,0:T(8,128)S(1)} %fusion.78), channel_id=2, replica_groups=mesh['dp'=8,'mp'=4] {'mp'}, dimensions={0}, use_global_device_ids=true | all-gather | bytes 983040 | tf_op jit(solution)/shard_map/all_gather | solution.py:86
  36.5 2.7 fusion.21
  39.9 5.7 convolution_bitcast_fusion
  45.6 12.0 %copy.103 = f32[4,16,16,16,16]{2,1,4,3,0:T(8,128)} copy(f32[4,16,16,16,16]{3,4,1,0,2:T(8,128)} %convolution_bitcast_fusion) | data formatting | bytes 2097152 | tf_op jit(solution)/shard_map/add | solution.py:49
  57.7 7.0 reshape.214
  64.7 54.7 %all-gather.7.cloned.1.call-done = bf16[8,256,1024]{2,1,0:T(8,128)(2,1)} async-done(((bf16[2,256,1024]{2,1,0:T(8,128)(2,1)}), bf16[8,256,1024]{2,1,0:T(8,128)(2,1)}) %all-gather.7.cloned.1.call-update) | async-done | bytes 4194320 | tf_op jit(solution)/shard_map/all_gather | solution.py:105
  119.4 6.1 convert_bitcast_fusion
  126.9 2.9 fusion.83
  129.8 1.7 exponential_reduce_fusion
  131.5 1.5 copy-done.1
  133.0 1.4 convolution_convert_fusion.4
  135.4 3.3 convolution_convert_fusion.1
  138.8 75.4 %reduce-scatter.5.cloned.1.call-done = bf16[2,256,1024]{2,1,0:T(8,128)(2,1)} async-done(((bf16[8,256,1024]{2,1,0:T(8,128)(2,1)}), bf16[2,256,1024]{2,1,0:T(8,128)(2,1)}) %reduce-scatter.5.cloned.1.call-update) | async-done | bytes 1048592 | tf_op jit(solution)/shard_map/reduce_scatter | solution.py:123
  214.2 2.1 fusion.40
  216.3 2.1 multiply_reduce_fusion.3
  218.4 1.6 add_convert_fusion.1
  220.1 2.5 multiply_convert_fusion.5
  222.7 78.7 %all-gather.9.cloned.1.call-done = bf16[8,256,1024]{2,1,0:T(8,128)(2,1)} async-done(((bf16[2,256,1024]{2,1,0:T(8,128)(2,1)}), bf16[8,256,1024]{2,1,0:T(8,128)(2,1)}) %all-gather.9.cloned.1.call-update) | async-done | bytes 4194320 | tf_op jit(solution)/shard_map/all_gather | solution.py:133
  301.5 10.9 fusion.34
  312.4 70.4 %all-gather.11.cloned.1.call-done = bf16[8,256,1024]{2,1,0:T(8,128)(2,1)} async-done(((bf16[2,256,1024]{2,1,0:T(8,128)(2,1)}), bf16[8,256,1024]{2,1,0:T(8,128)(2,1)}) %all-gather.11.cloned.1.call-update) | async-done | bytes 4194320 | tf_op jit(solution)/shard_map/all_gather | solution.py:149
  382.7 12.8 %fusion.6 = bf16[8,256,1024]{2,1,0:T(8,128)(2,1)S(1)} fusion(f32[8,256,1024]{2,1,0:T(8,128)} %fusion.34, bf16[8,256,1024]{2,1,0:T(8,128)(2,1)} %all-gather.11.cloned.1.call-done, bf16[1024,1024]{1,0:T(8,128)(2,1)} %param.19), kind=kOutput, calls=%fused_computation.8 | convolution fusion | flops 4336910336 | bytes 18874368 | tf_op jit(solution)/shard_map/wtd,fd->wtf/dot_general | solution.py:156
  395.5 2.0 copy-done.34
  397.5 7.0 fusion.32
  404.6 143.2 %reduce-scatter.9.cloned.1.call-done = f32[2,256,1024]{2,1,0:T(8,128)} async-done(((f32[8,256,1024]{2,1,0:T(8,128)}), f32[2,256,1024]{2,1,0:T(8,128)}) %reduce-scatter.9.cloned.1.call-update) | async-done | bytes 2097168 | tf_op jit(solution)/shard_map/reduce_scatter | solution.py:162
  547.8 3.3 multiply_reduce_fusion.1
  552.2 1.3 copy-done.6
  553.6 1.4 multiply_convert_fusion.4
  555.1 81.5 %all-gather.13.cloned.1.call-done = bf16[8,256,1024]{2,1,0:T(8,128)(2,1)} async-done(((bf16[2,256,1024]{2,1,0:T(8,128)(2,1)}), bf16[8,256,1024]{2,1,0:T(8,128)(2,1)}) %all-gather.13.cloned.1.call-update) | async-done | bytes 4194320 | tf_op jit(solution)/shard_map/all_gather | solution.py:173
  636.5 3.7 convolution_convert_fusion.3
  640.3 6.0 convolution_convert_fusion.2
  646.3 2.5 multiply_reduce_fusion
  648.8 3.9 convert_reduce_fusion
  652.7 2.4 multiply_convert_fusion.2
  655.1 1.8 multiply_convert_fusion.3
  656.9 2.3 copy.79
  659.1 2.3 copy.77
  661.4 2.3 copy.78
  663.7 7.8 bitcast_convert_fusion
  671.6 11.5 %convolution_convert_fusion = bf16[8,256,1024]{2,1,0:T(8,128)(2,1)} fusion(bf16[1024,1024]{1,0:T(8,128)(2,1)} %param.19, f32[8,256,1024]{2,1,0:T(8,128)} %fusion.34), kind=kOutput, calls=%fused_computation.34 | convolution fusion | flops 4315938816 | bytes 14680064 | tf_op jit(solution)/shard_map/wtf,fd->wtd/dot_general | solution.py:138
  683.4 10.2 convolution_bitcast_fusion.2
  693.6 11.2 convolution_bitcast_fusion.1
  704.8 2.3 convolution_bitcast_fusion.3
  708.4 5.5 fusion.36
  713.8 33.1 %reduce-scatter.11.cloned.1.call-done = bf16[2,256,1024]{2,1,0:T(8,128)(2,1)} async-done(((bf16[8,256,1024]{2,1,0:T(8,128)(2,1)}), bf16[2,256,1024]{2,1,0:T(8,128)(2,1)}) %reduce-scatter.11.cloned.1.call-update) | async-done | bytes 1048592 | tf_op jit(solution)/shard_map/reduce_scatter | solution.py:214
  747.0 1.4 reduce
  748.4 2.1 fusion.29
  750.5 2.7 fusion.27
  753.2 73.9 %reduce-scatter.7.cloned.1.call-done = bf16[2,256,1024]{2,1,0:T(8,128)(2,1)} async-done(((bf16[8,256,1024]{2,1,0:T(8,128)(2,1)}), bf16[2,256,1024]{2,1,0:T(8,128)(2,1)}) %reduce-scatter.7.cloned.1.call-update) | async-done | bytes 1048592 | tf_op jit(solution)/shard_map/reduce_scatter | solution.py:137
  827.2 5.2 fusion.26
  832.5 13.8 %all-gather.1 = bf16[4,2,6144]{2,1,0:T(2,128)(2,1)S(1)} all-gather(bf16[1,2,6144]{2,1,0:T(2,128)(2,1)S(1)} %bitcast.180), channel_id=1, replica_groups=mesh['dp'=8,'mp'=4] {'mp'}, dimensions={0}, use_global_device_ids=true | all-gather | bytes 122880 | tf_op jit(solution)/shard_map/all_gather | solution.py:236
  848.3 1.7 fusion.60
  850.0 3.7 fusion.77
  854.5 6.1 reshape.189
  860.6 6.9 convolution_bitcast_fusion.5
  868.1 25.8 %all-reduce = (f32[6,1024]{1,0:T(8,128)}, f32[4,961]{1,0:T(4,128)}) all-reduce(f32[6,1024]{1,0:T(8,128)S(1)} %reshape.188, f32[4,961]{1,0:T(4,128)S(1)} %reshape.190), channel_id=1, replica_groups=mesh['dp'=8,'mp'=4] {'dp'}, use_global_device_ids=true, to_apply=%region_28.29 | all-reduce | flops 9988 | bytes 79904 | tf_op jit(solution)/shard_map/psum | solution.py:255
  893.9 215.5 %all-reduce.4.cloned.1.call-done = (f32[3,1024,256]{1,2,0:T(8,128)}, f32[256,1024]{1,0:T(8,128)}, f32[1024,1024]{1,0:T(8,128)}, f32[1024,1024]{1,0:T(8,128)}, f3...) async-done(((f32[3,1024,256]{1,2,0:T(8,128)}, f32[256,1024]{1,0:T(8,128)}, f32[1024,1024]{1,0:T(8,128)}, f32[1024,1024]{1,0:T(8,128)}, ...) | async-done | bytes 20160528 | tf_op jit(solution)/shard_map/psum | solution.py:255
  1109.3 3.5 copy.85
  1112.9 2.3 copy.123
  1115.2 5.1 copy.124
  1120.3 2.1 copy.125
  1122.4 1.4 slice-done.3
  1123.8 2.7 copy.126
  (137 shorter events, 16.1 us)
Async XLA Ops:
  7.2 7.2 copy-start
  7.2 112.2 %all-gather.7.cloned.1.call-start = ((), (), s32[]{:S(2)}) async-start(), calls=%async_computation.4 | async-start | bytes 5242880 | tf_op jit(solution)/shard_map/all_gather | solution.py:105
  14.9 24.3 %copy-start.27 = (bf16[4,961]{1,0:T(4,128)(2,1)S(1)}, bf16[4,961]{1,0:T(4,128)(2,1)}, u32[]{:S(2)}) copy-start(bf16[4,961]{1,0:T(4,128)(2,1)} %param.24) | copy-start | bytes 23068
  39.1 175.0 %reduce-scatter.5.cloned.1.call-start = ((), (), s32[]{:S(2)}) async-start(), calls=%async_computation.5 | async-start | bytes 5242880 | tf_op jit(solution)/shard_map/reduce_scatter | solution.py:123
  39.3 0.6 copy-start.25
  57.7 7.0 copy-start.29
  125.5 1.4 copy-start.15
  125.8 4.0 copy-start.7
  125.8 4.0 copy-start.12
  125.8 5.7 copy-start.9
  129.8 3.2 copy-start.1
  133.0 2.4 copy-start.23
  134.4 1.0 copy-start.17
  138.7 162.7 %all-gather.9.cloned.1.call-start = ((), (), s32[]{:S(2)}) async-start(), calls=%async_computation.6 | async-start | bytes 5242880 | tf_op jit(solution)/shard_map/all_gather | solution.py:133
  214.2 4.2 copy-start.2
  214.2 4.2 copy-start.4
  220.1 162.7 %all-gather.11.cloned.1.call-start = ((), (), s32[]{:S(2)}) async-start(), calls=%async_computation.8 | async-start | bytes 5242880 | tf_op jit(solution)/shard_map/all_gather | solution.py:149
  222.7 325.1 %reduce-scatter.9.cloned.1.call-start = ((), (), s32[]{:S(2)}) async-start(), calls=%async_computation.9 | async-start | bytes 10485760 | tf_op jit(solution)/shard_map/reduce_scatter | solution.py:162
  382.7 14.8 %copy-start.33 = (bf16[1024,1024]{1,0:T(8,128)(2,1)S(1)}, bf16[1024,1024]{1,0:T(8,128)(2,1)}, u32[]{:S(2)}) copy-start(bf16[1024,1024]{1,0:T(8,128)(2,1)} %param.18) | copy-start | bytes 6291460
  395.5 2.0 copy-start.34
  404.5 232.0 %all-gather.13.cloned.1.call-start = ((), (), s32[]{:S(2)}) async-start(), calls=%async_computation.10 | async-start | bytes 5242880 | tf_op jit(solution)/shard_map/all_gather | solution.py:173
  547.8 3.3 copy-start.3
  547.8 3.4 copy-start.5
  547.8 3.5 copy-start.14
  551.3 2.3 copy-start.11
  552.2 1.4 copy-start.6
  555.0 191.9 %reduce-scatter.11.cloned.1.call-start = ((), (), s32[]{:S(2)}) async-start(), calls=%async_computation.11 | async-start | bytes 5242880 | tf_op jit(solution)/shard_map/reduce_scatter | solution.py:214
  636.5 9.7 slice-start
  640.3 6.0 slice-start.1
  640.3 6.0 copy-start.10
  648.8 3.9 copy-start.13
  652.7 2.4 copy-start.8
  671.5 155.6 %reduce-scatter.7.cloned.1.call-start = ((), (), s32[]{:S(2)}) async-start(), calls=%async_computation.7 | async-start | bytes 5242880 | tf_op jit(solution)/shard_map/reduce_scatter | solution.py:137
  683.1 426.2 %all-reduce.4.cloned.1.call-start = ((), (), s32[]{:S(2)}) async-start(), calls=%async_computation.12 | async-start | bytes 40321024 | tf_op jit(solution)/shard_map/psum | solution.py:255
  683.4 10.2 copy-start.31
  693.6 11.2 copy-start.18
  693.6 11.2 copy-start.32
  704.8 2.3 copy-start.19
  704.8 2.3 copy-start.20
  704.8 2.3 copy-start.21
  704.8 3.6 copy-start.30
  832.4 15.9 %copy-start.28 = (s32[8]{0:T(128)S(1)}, s32[8]{0:T(128)}, u32[]{:S(2)}) copy-start(s32[8]{0:T(128)} %param.26) | copy-start | bytes 100
  853.7 0.7 copy-start.26
  1115.2 5.1 copy-start.16
  1115.2 7.2 slice-start.2
  1120.3 3.5 slice-start.3
  1123.8 2.7 copy-start.24
  1123.8 3.4 copy-start.22
Sparse Core Ops, SparseCore 0:
  39.3 80.0 all-gather.6
  138.9 75.2 reduce-scatter.4
  220.2 81.2 all-gather.8
  303.5 79.2 all-gather.10
  404.6 143.0 reduce-scatter.8
  555.2 81.3 all-gather.12
  671.6 75.2 reduce-scatter.10
  749.8 77.2 reduce-scatter.6
  853.8 255.4 all-reduce.3
